TPU v7x, 32 devices: a whole 2x2x4 slice. The times are simulated.
32 devices in a mesh: groups: 2 (over y), ctx: 4 (over z), head: 2 (over x), sess: 2 (over core).
Axes of the slice: x: 2, y: 2, z: 4, core: 2. Of those that a mesh axis runs over, the one named last changes fastest.
Arguments:
- head_input: bfloat16 [8, 512, 8192], P(('groups', 'sess'), 'ctx', 'head'), parts along dimension 0, may hold values from -6 to 6
- gate_input: bfloat16 [8, 512, 8192], P(('groups', 'sess'), 'ctx', 'head'), parts along dimension 0, may hold values from -6 to 6
- state_in_proj: bfloat16 [8, 512, 8, 128], P(('groups', 'sess'), 'ctx'), parts along dimension 0, may hold values from -1.796875 to 1.796875
- state_out_proj: bfloat16 [8, 512, 8, 128], P(('groups', 'sess'), 'ctx'), parts along dimension 0, may hold values from -1.796875 to 1.796875
- step_raw: float32 [8, 512, 128], P(('groups', 'sess'), 'ctx', 'head'), parts along dimension 0, may hold values from -2.5 to 12.5
- head_step_bias: float32 [128], P('head'), may hold values from -5.3 to -2.25
- decay_log: float32 [128], P('head'), may hold values from -7.7 to 0
- skip_gain: float32 [128], P('head'), may hold values from 0.5 to 2
- norm_gain: float32 [8192], P('head'), may hold values from 0.1 to 1.9
- out_weight: bfloat16 [8192, 4096], P('head', 'ctx'), may hold values from -0.09375 to 0.09375
- pool_states: float32 [16, 128, 64, 128], P(('groups', 'sess'), 'head', None, 'ctx'), parts along dimension 0, may hold values from -6 to 6
- slot_map: int32 [8], P('groups'), parts along dimension 0, may hold values from 0 to 7, as said below
- span_lengths: int32 [8], P('groups'), parts along dimension 0, may hold values from 1 to 4, as said below
Outputs:
- mixed: bfloat16 [8, 512, 4096], P(('groups', 'sess'), 'ctx', 'head'), parts along dimension 0
- final_states: float32 [8, 128, 64, 128], P(('groups', 'sess'), 'head', None, 'ctx'), parts along dimension 0
There are 2 independent parts, one for each index of `groups`. A program takes and returns all parts, laid end to end along the dimension named above; an argument that names none is the same for every part. Nothing has to cross between parts.
Inputs may be any that keep to these rules, and one draw needn't show every extreme that they name: `slot_map`: the sessions of a group take distinct decode slots. `span_lengths`: some session of every group fills all 4 units.
All inputs are finite; a program needn't handle non-finite values.
Results may differ from a plain program's by a relative error of at most 0.018.
Values may be sent and summed in bfloat16 or wider, within the bound.
A program may use at most 128 MiB of HBM per device.

v0:
```python
import jax
import jax.numpy as jnp
from jax import lax
from jax.sharding import PartitionSpec as P

HEADS = 128
GROUPS = 8
SPAN = 128
highest = lax.Precision.HIGHEST
norm_eps = 1e-05


def shifted(value, axis, by):
    length = lax.axis_size(axis)
    pairs = [(i, i + by) for i in range(length) if 0 <= i + by < length]
    return lax.ppermute(value, axis, pairs)


def from_root(block, axis, owner):
    block = jnp.where(lax.axis_index(axis) == owner, block, jnp.zeros_like(block))
    return lax.psum(block, axis)


def shards(
    head_input,
    gate_input,
    state_in_proj,
    state_out_proj,
    step_raw,
    head_step_bias,
    decay_log,
    skip_gain,
    norm_gain,
    out_weight,
    pool_states,
    slot_map,
    span_lengths,
):
    ctx_count = lax.axis_size("ctx")
    ctx_index = lax.axis_index("ctx")
    sess_index = lax.axis_index("sess")
    head_index = lax.axis_index("head")
    sessions, tokens, inner = head_input.shape
    heads = step_raw.shape[2]
    head_dim = inner // heads
    state_cols = pool_states.shape[3]
    group_heads = HEADS // GROUPS
    spans = tokens // SPAN
    first_session = sess_index * sessions
    own_lengths = lax.dynamic_slice_in_dim(span_lengths, first_session, sessions)
    position = ctx_index * tokens + jnp.arange(tokens, dtype=jnp.int32)
    live_rows = (position[None, :] < own_lengths[:, None] * SPAN).astype(jnp.float32)
    step_size = jax.nn.softplus(step_raw + head_step_bias) * live_rows[:, :, None]
    log_keep = -jnp.exp(decay_log) * step_size
    pooled = lax.all_gather(pool_states.astype(jnp.bfloat16), "sess", axis=0, tiled=True).astype(
        pool_states.dtype
    )
    own_slots = lax.dynamic_slice_in_dim(slot_map, first_session, sessions)
    start_cols = jnp.take(pooled, own_slots, axis=0)
    start_state = lax.all_gather(start_cols.astype(jnp.bfloat16), "ctx", axis=3, tiled=True).astype(
        start_cols.dtype
    )
    first_head = head_index * heads
    group_count = max(1, heads // group_heads)
    repeats = min(heads, group_heads)
    first_group = first_head // group_heads
    state_size = state_in_proj.shape[3]
    group_shape = (sessions, spans, SPAN, group_count, state_size)
    b_groups = (
        lax.dynamic_slice_in_dim(state_in_proj, first_group, group_count, 2)
        .astype(jnp.float32)
        .reshape(group_shape)
    )
    c_groups = (
        lax.dynamic_slice_in_dim(state_out_proj, first_group, group_count, 2)
        .astype(jnp.float32)
        .reshape(group_shape)
    )
    b_heads = jnp.repeat(b_groups, repeats, axis=3)
    c_heads = jnp.repeat(c_groups, repeats, axis=3)
    inputs = head_input.astype(jnp.float32).reshape(sessions, spans, SPAN, heads, head_dim)
    cum_log = jnp.cumsum(log_keep.reshape(sessions, spans, SPAN, heads), axis=2)
    cum_heads = jnp.moveaxis(cum_log, 3, 2)
    size_heads = jnp.moveaxis(step_size.reshape(sessions, spans, SPAN, heads), 3, 2)
    causal = jnp.arange(SPAN)[:, None] >= jnp.arange(SPAN)[None, :]
    log_gap = cum_heads[..., :, None] - cum_heads[..., None, :]
    decay_pairs = (
        jnp.where(causal, jnp.exp(jnp.where(causal, log_gap, 0.0)), 0.0) * size_heads[..., None, :]
    )
    products_cb = jnp.einsum("sclgn,scmgn->scglm", c_groups, b_groups, precision=highest)
    score_values = jnp.repeat(products_cb, repeats, axis=2) * decay_pairs
    inside_span = jnp.einsum("schlm,scmhp->sclhp", score_values, inputs, precision=highest)
    tail_weight = jnp.exp(cum_heads[..., -1:] - cum_heads) * size_heads
    span_states = jnp.einsum(
        "schm,scmhp,scmhn->schpn", tail_weight, inputs, b_heads, precision=highest
    )
    span_log = cum_heads[..., -1]
    running = jnp.zeros((sessions, heads, head_dim, state_size), jnp.float32)
    entering = [running]
    running = jnp.exp(span_log[:, 0])[..., None, None] * running + span_states[:, 0]
    local_end = running
    shard_log = jnp.sum(span_log, axis=1)
    entry_states = jnp.stack(entering, axis=1)
    prior_log = jnp.cumsum(span_log, axis=1) - span_log
    from_entry = (
        jnp.einsum("sclhn,schpn->sclhp", c_heads, entry_states, precision=highest)
        * jnp.exp(cum_log)[..., None]
    )

    def relay_turn(turn_index, carried):
        outgoing = jnp.exp(shard_log)[..., None, None] * carried + local_end
        incoming = shifted(outgoing.astype(jnp.bfloat16), "ctx", 1).astype(outgoing.dtype)
        return jnp.where(ctx_index == 0, start_state, incoming)

    carried = lax.fori_loop(0, ctx_count - 1, relay_turn, start_state)
    from_start = cum_log + prior_log[:, :, None, :]
    from_carry = (
        jnp.einsum("sclhn,shpn->sclhp", c_heads, carried, precision=highest)
        * jnp.exp(from_start)[..., None]
    )
    ssd_out = inside_span + from_entry + from_carry + skip_gain[:, None] * inputs
    gated = ssd_out.reshape(sessions, tokens, inner) * jax.nn.silu(gate_input.astype(jnp.float32))
    grouped = gated.reshape(sessions, tokens, heads // group_heads, group_heads * head_dim)
    norm_scale = lax.rsqrt(jnp.mean(grouped * grouped, axis=3, keepdims=True) + norm_eps)
    normed = (grouped * norm_scale).reshape(sessions, tokens, inner)
    normed = (normed * norm_gain).astype(jnp.bfloat16)
    partial_out = jnp.einsum(
        "stk,kd->std",
        normed,
        lax.all_gather(out_weight, "ctx", axis=1, tiled=True),
        preferred_element_type=jnp.float32,
    )
    summed = lax.psum_scatter(
        partial_out.astype(jnp.bfloat16), "head", scatter_dimension=2, tiled=True
    ).astype(jnp.float32)
    mixed = (summed * live_rows[:, :, None]).astype(jnp.bfloat16)
    end_state = jnp.exp(shard_log)[..., None, None] * carried + local_end
    whole_end = from_root(end_state.astype(jnp.bfloat16), "ctx", ctx_count - 1).astype(
        end_state.dtype
    )
    final_states = lax.dynamic_slice_in_dim(whole_end, ctx_index * state_cols, state_cols, 3)
    return (mixed, final_states)


def solution(mesh):
    placed = (
        P(("groups", "sess"), "ctx", "head"),
        P(("groups", "sess"), "ctx", "head"),
        P(("groups", "sess"), "ctx", None, None),
        P(("groups", "sess"), "ctx", None, None),
        P(("groups", "sess"), "ctx", "head"),
        P("head"),
        P("head"),
        P("head"),
        P("head"),
        P("head", "ctx"),
        P(("groups", "sess"), "head", None, "ctx"),
        P("groups"),
        P("groups"),
    )
    return jax.shard_map(
        shards,
        mesh=mesh,
        in_specs=placed,
        out_specs=(
            P(("groups", "sess"), "ctx", "head"),
            P(("groups", "sess"), "head", None, "ctx"),
        ),
        check_vma=False,
    )
```

profile of v0, /device:TPU:0, one launch (start us, length us, event | category | flops | bytes accessed | tf_op | source)
XLA Modules:
  0.0 939.3 jit_solution(13627045292249434513)
XLA Ops:
  7.2 4.0 convert_element_type.59
  11.4 16.4 %all-gather.4.cloned.1.call-done = bf16[8,64,64,32]{2,3,1,0:T(8,128)(2,1)} async-done(((bf16[4,64,64,32]{2,3,1,0:T(8,128)(2,1)}), bf16[8,64,64,32]{2,3,1,0:T(8,128)(2,1)}) %all-gather.4.cloned.1.call-update) | async-done | bytes 2097168 | tf_op jit(solution)/shard_map/all_gather | solution.py:55
  27.8 2.9 gather_fusion
  30.7 1.2 select_convert_fusion
  32.1 0.7 all-gather.8.cloned.1.call-update
  32.8 0.8 copy-done.1
  33.6 2.4 copy.86
  36.1 3.0 copy.92
  40.3 0.3 constant_dynamic-slice_fusion
  40.7 0.3 fusion.35
  41.0 1.1 broadcast_in_dim.68
  42.0 17.8 %fusion.33 = f32[2,64,64,128]{3,2,1,0:T(8,128)} fusion(f32[2,128,64,128]{3,1,2,0:T(8,128)S(1)} %bitcast.69), kind=kOutput, calls=%fused_computation.41 | convolution fusion | flops 1610612736 | bytes 12582912 | tf_op jit(solution)/shard_map/sclhn,schpn->sclhp/dot_general | solution.py:106
  59.8 1.1 broadcast_in_dim.74
  60.9 0.5 copy-done.2
  61.4 9.1 fusion.27
  70.5 1.0 broadcast_in_dim.64
  71.6 11.9 %fusion.2 = f32[2,64,128,64]{2,3,1,0:T(8,128)} fusion(bf16[2,128,64,64]{1,3,2,0:T(8,128)(2,1)S(1)} %bitcast.76, f32[2,64,128,128]{3,2,1,0:T(8,128)S(1)} %bitcast.74, f32[2,64,128]{2,1,0:T(8,128)S(1)} %copy.85, f32[2,64,128]{2,1,0:T(8,128)S(1)} %copy.83, pred[128,128]{1,0:T(8,128)(4,1)S(1)} %iota_compare_fusion), kind=kOutput, calls=%fused_computation.5 | convolution fusion | flops 1621098496 | bytes 14827520 | tf_op jit(solution)/shard_map/schlm,scmhp->sclhp/dot_general | solution.py:92
  83.5 30.6 %all-gather.6.cloned.1.call-done = bf16[2,64,64,128]{2,3,1,0:T(8,128)(2,1)} async-done(((bf16[2,64,64,32]{2,3,1,0:T(8,128)(2,1)}), bf16[2,64,64,128]{2,3,1,0:T(8,128)(2,1)}) %all-gather.6.cloned.1.call-update) | async-done | bytes 2097168 | tf_op jit(solution)/shard_map/all_gather | solution.py:60
  114.1 5.2 copy.89
  119.3 6.7 copy.107
  125.9 393.2 %while.12 = (s32[]{:T(128)}, f32[2,64,64,128]{3,2,1,0:T(8,128)}, pred[]{:T(512)}, f32[2,64,1,1]{1,0,3,2:T(2,128)S(1)}, f32[2,64,64,128]{3,2,1,0:T(8,128)}, /*index=5*/f32[2,64,64,128]{3,2,1,0:T(8,128)}, s32[]{:T(128)}) while((s32[]{:T(128)}, f32[2,64,64,128]{3,2,1,0:T(8,128)}, pred[]{:T(512)}, f32[2,64,1,1]{1,0,3,2:T(2,128)S(1)}, ...), condition=%wide.region_2.3_spmd, body=%wide.region_1.2_spmd.sunk | while | flops 5242882 | bytes 29360756 | solution.py:115
  125.9 5.7 add_convert_fusion.3
  131.6 2.6 collective-permute-start
  134.2 89.2 %collective-permute-done = bf16[2,64,64,128]{3,2,1,0:T(8,128)(2,1)} collective-permute-done((bf16[2,64,64,128]{3,2,1,0:T(8,128)(2,1)S(1)}, bf16[2,64,64,128]{3,2,1,0:T(8,128)(2,1)}, u32[]{:S(2)}, u32[]{:S(2)}) %collective-permute-start) | collective-permute-done | bytes 2097184 | tf_op jit(solution)/shard_map/while/body/eval_jaxpr/ppermute | solution.py:16
  223.4 5.9 convert_select_fusion.2
  229.3 4.1 add_convert_fusion.3
  233.4 46.4 %collective-permute-start = (bf16[2,64,64,128]{3,2,1,0:T(8,128)(2,1)S(1)}, bf16[2,64,64,128]{3,2,1,0:T(8,128)(2,1)}, u32[]{:S(2)}, u32[]{:S(2)}) collective-permute-start(bf16[2,64,64,128]{3,2,1,0:T(8,128)(2,1)S(1)} %add_convert_fusion.3), channel_id=1, source_target_pairs={{0,4},{4,8},{8,12},{1,5},{5,9},{9,13},{2,6},{6,10},{10,14},{3,7},{... | collective-permute-start | bytes 6291464 | tf_op jit(solution)/shard_map/while/body/eval_jaxpr/ppermute | solution.py:16
  279.8 88.9 %collective-permute-done = bf16[2,64,64,128]{3,2,1,0:T(8,128)(2,1)} collective-permute-done((bf16[2,64,64,128]{3,2,1,0:T(8,128)(2,1)S(1)}, bf16[2,64,64,128]{3,2,1,0:T(8,128)(2,1)}, u32[]{:S(2)}, u32[]{:S(2)}) %collective-permute-start) | collective-permute-done | bytes 2097184 | tf_op jit(solution)/shard_map/while/body/eval_jaxpr/ppermute | solution.py:16
  368.7 5.9 convert_select_fusion.2
  374.7 4.0 add_convert_fusion.3
  378.7 49.8 %collective-permute-start = (bf16[2,64,64,128]{3,2,1,0:T(8,128)(2,1)S(1)}, bf16[2,64,64,128]{3,2,1,0:T(8,128)(2,1)}, u32[]{:S(2)}, u32[]{:S(2)}) collective-permute-start(bf16[2,64,64,128]{3,2,1,0:T(8,128)(2,1)S(1)} %add_convert_fusion.3), channel_id=1, source_target_pairs={{0,4},{4,8},{8,12},{1,5},{5,9},{9,13},{2,6},{6,10},{10,14},{3,7},{... | collective-permute-start | bytes 6291464 | tf_op jit(solution)/shard_map/while/body/eval_jaxpr/ppermute | solution.py:16
  428.4 84.8 %collective-permute-done = bf16[2,64,64,128]{3,2,1,0:T(8,128)(2,1)} collective-permute-done((bf16[2,64,64,128]{3,2,1,0:T(8,128)(2,1)S(1)}, bf16[2,64,64,128]{3,2,1,0:T(8,128)(2,1)}, u32[]{:S(2)}, u32[]{:S(2)}) %collective-permute-start) | collective-permute-done | bytes 2097184 | tf_op jit(solution)/shard_map/while/body/eval_jaxpr/ppermute | solution.py:16
  513.2 5.9 convert_select_fusion.2
  519.1 22.6 %fusion.17 = f32[2,1,128,64,64]{2,4,3,0,1:T(8,128)} fusion(f32[2,64,64,128]{3,2,1,0:T(8,128)} %fusion.33, f32[2,64,128,64]{2,3,1,0:T(8,128)} %fusion.2, f32[2,1,128,64,64]{2,4,3,0,1:T(8,128)} %bitcast.72, f32[2,64,64,128]{3,2,1,0:T(8,128)} %get-tuple-element.76, f32[2,128,64,128]{3,1,2,0:T(8,128)} %bitcast.70, f32[64]{0:T(128)S(1)} %copy-done.8, ...), kind=kOutput, calls=%fused_computation.21 | convolution fusion | flops 1616904192 | bytes 29491456 | tf_op jit(solution)/shard_map/sclhn,shpn->sclhp/dot_general | solution.py:118
  541.7 5.8 copy.93
  547.5 5.3 fusion.45
  552.9 6.0 mul.183
  558.9 2.8 reduce_sum.8
  561.7 2.6 mul.184
  564.3 6.1 mul.185
  570.4 5.5 fusion.30
  576.0 230.1 %all-gather.8.cloned.1.call-done = bf16[4096,4096]{1,0:T(8,128)(2,1)} async-done(((bf16[4096,1024]{1,0:T(8,128)(2,1)}), bf16[4096,4096]{1,0:T(8,128)(2,1)}) %all-gather.8.cloned.1.call-update) | async-done | bytes 33554448 | tf_op jit(solution)/shard_map/all_gather | solution.py:130
  806.0 19.4 %fusion.9 = bf16[2,128,4096]{2,1,0:T(8,128)(2,1)} fusion(bf16[4096,4096]{1,0:T(8,128)(2,1)} %all-gather.8.cloned.1.call-done, f32[2,128,4096]{2,1,0:T(8,128)} %mul.185, f32[4096]{0:T(1024)S(1)} %copy-done.10, f32[2,128,4096]{2,1,0:T(8,128)} %copy.93, bf16[2,128,4096]{2,1,0:T(8,128)(2,1)S(1)} %copy-done.3), kind=kOutput, calls=%fused_computation.14 | convolution fusion | flops 8600420352 | bytes 46153728 | tf_op jit(solution)/shard_map/stk,kd->std/dot_general | solution.py:127
  825.5 71.8 %all-reduce.2.cloned.1.call-done = bf16[2,64,64,128]{3,2,1,0:T(8,128)(2,1)} async-done(((bf16[2,64,64,128]{3,2,1,0:T(8,128)(2,1)}), bf16[2,64,64,128]{3,2,1,0:T(8,128)(2,1)}) %all-reduce.2.cloned.1.call-update) | async-done | bytes 2097168 | tf_op jit(solution)/shard_map/psum | solution.py:21
  897.2 4.3 dynamic-slice_convert_fusion
  901.5 3.8 copy.96
  905.3 25.0 %reduce-scatter.2.cloned.1.call-done = bf16[2,128,2048]{2,1,0:T(8,128)(2,1)} async-done(((bf16[2,128,4096]{2,1,0:T(8,128)(2,1)}), bf16[2,128,2048]{2,1,0:T(8,128)(2,1)}) %reduce-scatter.2.cloned.1.call-update) | async-done | bytes 1048592 | tf_op jit(solution)/shard_map/reduce_scatter | solution.py:133
  930.3 2.4 multiply_convert_fusion.2
  (55 shorter events, 1.6 us)
Async XLA Ops:
  7.2 4.1 copy-start.9
  7.2 20.6 %all-gather.4.cloned.1.call-start = ((), (), s32[]{:S(2)}) async-start(), calls=%async_computation.1 | async-start | bytes 6291456 | tf_op jit(solution)/shard_map/all_gather | solution.py:55
  11.2 102.8 %all-gather.6.cloned.1.call-start = ((), (), s32[]{:S(2)}) async-start(), calls=%async_computation.2 | async-start | bytes 5242880 | tf_op jit(solution)/shard_map/all_gather | solution.py:60
  32.0 1.6 copy-start.1
  32.0 774.0 %all-gather.8.cloned.1.call-start = ((), (), s32[]{:S(2)}) async-start(), calls=%async_computation.3 | async-start | bytes 41943040 | tf_op jit(solution)/shard_map/all_gather | solution.py:130
  32.8 864.5 %all-reduce.2.cloned.1.call-start = ((), (), s32[]{:S(2)}) async-start(), calls=%async_computation.5 | async-start | bytes 4194304 | tf_op jit(solution)/shard_map/psum | solution.py:21
  36.0 3.0 copy-start.6
  36.0 3.1 copy-start.11
  36.0 3.2 copy-start.12
  36.0 3.3 copy-start.7
  36.0 4.2 copy-start.4
  36.1 4.2 copy-start.5
  42.0 17.8 %copy-start = (f32[2,128,4,16,128]{4,1,3,2,0:T(8,128)}, f32[2,128,4,16,128]{4,1,3,2,0:T(8,128)S(1)}, u32[]{:S(2)}) copy-start(f32[2,128,4,16,128]{4,1,3,2,0:T(8,128)S(1)} %broadcast_in_dim.68) | copy-start | bytes 25165828
  59.8 1.6 copy-start.2
  125.9 393.2 %copy-start.8 = (f32[64]{0:T(128)S(1)}, f32[64]{0:T(128)}, u32[]{:S(2)}) copy-start(f32[64]{0:T(128)} %param.22) | copy-start | bytes 772
  131.6 91.8 %collective-permute-start = (bf16[2,64,64,128]{3,2,1,0:T(8,128)(2,1)S(1)}, bf16[2,64,64,128]{3,2,1,0:T(8,128)(2,1)}, u32[]{:S(2)}, u32[]{:S(2)}) collective-permute-start(bf16[2,64,64,128]{3,2,1,0:T(8,128)(2,1)S(1)} %add_convert_fusion.3), channel_id=1, source_target_pairs={{0,4},{4,8},{8,12},{1,5},{5,9},{9,13},{2,6},{6,10},{10,14},{3,7},{... | collective-permute-start | bytes 6291464 | tf_op jit(solution)/shard_map/while/body/eval_jaxpr/ppermute | solution.py:16
  233.4 135.3 %collective-permute-start = (bf16[2,64,64,128]{3,2,1,0:T(8,128)(2,1)S(1)}, bf16[2,64,64,128]{3,2,1,0:T(8,128)(2,1)}, u32[]{:S(2)}, u32[]{:S(2)}) collective-permute-start(bf16[2,64,64,128]{3,2,1,0:T(8,128)(2,1)S(1)} %add_convert_fusion.3), channel_id=1, source_target_pairs={{0,4},{4,8},{8,12},{1,5},{5,9},{9,13},{2,6},{6,10},{10,14},{3,7},{... | collective-permute-start | bytes 6291464 | tf_op jit(solution)/shard_map/while/body/eval_jaxpr/ppermute | solution.py:16
  378.7 134.6 %collective-permute-start = (bf16[2,64,64,128]{3,2,1,0:T(8,128)(2,1)S(1)}, bf16[2,64,64,128]{3,2,1,0:T(8,128)(2,1)}, u32[]{:S(2)}, u32[]{:S(2)}) collective-permute-start(bf16[2,64,64,128]{3,2,1,0:T(8,128)(2,1)S(1)} %add_convert_fusion.3), channel_id=1, source_target_pairs={{0,4},{4,8},{8,12},{1,5},{5,9},{9,13},{2,6},{6,10},{10,14},{3,7},{... | collective-permute-start | bytes 6291464 | tf_op jit(solution)/shard_map/while/body/eval_jaxpr/ppermute | solution.py:16
  541.7 5.8 copy-start.3
  570.4 235.6 %copy-start.10 = (f32[4096]{0:T(1024)S(1)}, f32[4096]{0:T(1024)}, u32[]{:S(2)}) copy-start(f32[4096]{0:T(1024)} %param.23) | copy-start | bytes 49156
  575.9 354.4 %reduce-scatter.2.cloned.1.call-start = ((), (), s32[]{:S(2)}) async-start(), calls=%async_computation.4 | async-start | bytes 3145728 | tf_op jit(solution)/shard_map/reduce_scatter | solution.py:133
Sparse Core Ops, SparseCore 0:
  11.4 16.3 all-gather.3
  32.1 81.9 all-gather.5
  115.7 690.3 all-gather.7
  808.8 88.3 all-reduce.1
  899.3 30.9 reduce-scatter.1
where the time goes:
time: 940 us; the launch traced here: 939 us
  waiting for transfers between devices  637 us (68%)
  starting transfers between devices  99.1 us (11%)
  matrix products  81.1 us (9%)
  other arithmetic  57.8 us (6%)
  local copies, waits for them, and re-layouts  49.8 us (5%)
  between operations  14 us (1%)
    ppermute x3, waiting for transfers between devices, shifted(): return lax.ppermute(value, axis, pairs)  263 us
    all_gather x1, waiting for transfers between devices, shards(): lax.all_gather(out_weight, 'ctx', axis=1, tiled=True)  230 us
    ppermute x3, starting transfers between devices, shifted(): return lax.ppermute(value, axis, pairs)  98.8 us
    psum x1, waiting for transfers between devices, from_root(): return lax.psum(block, axis)  71.8 us
    all_gather x1, waiting for transfers between devices, shards(): lax.all_gather(start_cols.astype(jnp.bfloat16), 'ctx', axis=3, tiled=True)  30.6 us
    reduce_scatter x1, waiting for transfers between devices, shards(): lax.psum_scatter(partial_out.astype(jnp.bfloat16), 'head', scatter_dimens...  25 us
    dot_general x1, matrix products, shards(): jnp.einsum('sclhn,shpn->sclhp', c_heads, carried, precision=highest)  22.6 us
    dot_general x1, matrix products, shards(): jnp.einsum('stk,kd->std', normed, lax.all_gather(out_weight, 'ctx', axis=...  19.4 us
  transfers between devices with their start and end apart: 8, of which 8 were waited for; matrix products, arithmetic and copies ran while one was open for 19% of the time, Pallas kernels for 0%

commit v1 on v0

--- a/solution.py
+++ b/solution.py
@@ -127,7 +127,9 @@
     partial_out = jnp.einsum(
         "stk,kd->std",
         normed,
-        lax.all_gather(out_weight, "ctx", axis=1, tiled=True),
+        jnp.concatenate(
+            lax.all_to_all(jnp.stack([out_weight] * lax.axis_size("ctx")), "ctx", 0, 0), axis=1
+        ),
         preferred_element_type=jnp.float32,
     )
     summed = lax.psum_scatter(

time: 940 us -> 1200 us (1.28)
  local copies, waits for them, and re-layouts: 49.8 us -> 157 us
  starting transfers between devices: 99.1 us -> 201 us
  waiting for transfers between devices: 637 us -> 686 us
    all_gather x1 -> x0, waiting for transfers between devices: 230 us -> none  [shards(): lax.all_gather(out_weight, 'ctx', axis=1, tiled=True)]
    all_gather x1, waiting for transfers between devices: 30.6 us -> 218 us  [shards(): lax.all_gather(start_cols.astype(jnp.bfloat16), 'ctx', axis=3, tiled=True)]
    ppermute x3, waiting for transfers between devices: 263 us -> 434 us  [shifted(): return lax.ppermute(value, axis, pairs)]
    reshape x0 -> x2, local copies, waits for them, and re-layouts: none -> 96.2 us  [shards(): jnp.concatenate(lax.all_to_all(jnp.stack([out_weight] * lax.axis_size('ct...]
    ppermute x3, starting transfers between devices: 98.8 us -> 191 us  [shifted(): return lax.ppermute(value, axis, pairs)]
    psum x1, waiting for transfers between devices: 71.8 us -> 0.02 us  [from_root(): return lax.psum(block, axis)]
    another operation x1 -> x2, local copies, waits for them, and re-layouts: 0.08 us -> 13.6 us  [the longest x1 13.5 us: shards(): jnp.stack([out_weight] * lax.axis_size('ctx'))]
  transfers between devices with their start and end apart: 8 -> 8, of which waited for: 8 -> 6; matrix products, arithmetic and copies ran while one was open for 19% -> 23% of each run, Pallas kernels for 0% -> 0%
where the time goes in v1:
time: 1200 us
  waiting for transfers between devices  686 us (57%)
  starting transfers between devices  201 us (17%)
  local copies, waits for them, and re-layouts  157 us (13%)
  matrix products  81.5 us (7%)
  other arithmetic  56.4 us (5%)
  between operations  14.3 us (1%)
    ppermute x3, waiting for transfers between devices, shifted(): return lax.ppermute(value, axis, pairs)  434 us
    all_gather x1, waiting for transfers between devices, shards(): lax.all_gather(start_cols.astype(jnp.bfloat16), 'ctx', axis=3, tiled=True)  218 us
    ppermute x3, starting transfers between devices, shifted(): return lax.ppermute(value, axis, pairs)  191 us
    reshape x2, local copies, waits for them, and re-layouts, shards(): jnp.concatenate(lax.all_to_all(jnp.stack([out_weight] * lax.axis_size('ct...  96.2 us
    reduce_scatter x1, waiting for transfers between devices, shards(): lax.psum_scatter(partial_out.astype(jnp.bfloat16), 'head', scatter_dimens...  24.6 us
  transfers between devices with their start and end apart: 8, of which 6 were waited for; matrix products, arithmetic and copies ran while one was open for 23% of the time, Pallas kernels for 0%

profile of v1, /device:TPU:0, one launch (start us, length us, event | category | flops | bytes accessed | tf_op | source)
XLA Modules:
  0.0 1196.8 jit_solution(221705594596952937)
XLA Ops:
  7.2 13.5 %stack.2 = bf16[4,4096,1024]{2,1,0:T(8,128)(2,1)} broadcast(bf16[4096,1024]{1,0:T(8,128)(2,1)} %param.24), dimensions={1,2} | broadcast | bytes 41943040 | tf_op jit(solution)/shard_map/stack | solution.py:131
  20.6 9.7 all-to-all-start
  30.5 4.1 convert_element_type.59
  34.7 2.5 copy.88
  37.2 3.0 copy.94
  41.3 10.1 all-gather.3.cloned.1.call-done
  51.3 2.9 gather_fusion
  54.2 1.2 select_convert_fusion
  55.8 0.3 constant_dynamic-slice_fusion
  56.2 0.3 fusion.30
  56.5 1.1 broadcast_in_dim.68
  57.6 18.2 %fusion.28 = f32[2,64,64,128]{3,2,1,0:T(8,128)} fusion(f32[2,128,64,128]{3,1,2,0:T(8,128)S(1)} %bitcast.66), kind=kOutput, calls=%fused_computation.39 | convolution fusion | flops 1610612736 | bytes 12582912 | tf_op jit(solution)/shard_map/sclhn,schpn->sclhp/dot_general | solution.py:106
  75.8 1.1 broadcast_in_dim.74
  76.9 0.5 copy-done.2
  77.4 9.4 fusion.22
  86.8 1.1 broadcast_in_dim.64
  87.9 12.0 fusion
  99.8 217.8 %all-gather.5.cloned.1.call-done = bf16[2,64,64,128]{2,3,1,0:T(8,128)(2,1)} async-done(((bf16[2,64,64,32]{2,3,1,0:T(8,128)(2,1)}), bf16[2,64,64,128]{2,3,1,0:T(8,128)(2,1)}) %all-gather.5.cloned.1.call-update) | async-done | bytes 2097168 | tf_op jit(solution)/shard_map/all_gather | solution.py:60
  317.6 5.2 copy.91
  322.9 4.8 copy.110
  327.6 654.9 %while.12 = (s32[]{:T(128)}, f32[2,64,64,128]{3,2,1,0:T(8,128)}, pred[]{:T(512)}, f32[2,64,1,1]{1,0,3,2:T(2,128)S(1)}, f32[2,64,64,128]{3,2,1,0:T(8,128)}, /*index=5*/f32[2,64,64,128]{3,2,1,0:T(8,128)}, s32[]{:T(128)}) while((s32[]{:T(128)}, f32[2,64,64,128]{3,2,1,0:T(8,128)}, pred[]{:T(512)}, f32[2,64,1,1]{1,0,3,2:T(2,128)S(1)}, ...), condition=%wide.region_2.3_spmd, body=%wide.region_1.2_spmd.sunk | while | flops 5242882 | bytes 29360756 | solution.py:115
  327.8 4.0 add_convert_fusion.3
  331.8 2.6 collective-permute-start
  334.4 348.7 %collective-permute-done = bf16[2,64,64,128]{3,2,1,0:T(8,128)(2,1)} collective-permute-done((bf16[2,64,64,128]{3,2,1,0:T(8,128)(2,1)S(1)}, bf16[2,64,64,128]{3,2,1,0:T(8,128)(2,1)}, u32[]{:S(2)}, u32[]{:S(2)}) %collective-permute-start) | collective-permute-done | bytes 2097184 | tf_op jit(solution)/shard_map/while/body/eval_jaxpr/ppermute | solution.py:16
  683.2 5.9 convert_select_fusion.2
  689.1 4.0 add_convert_fusion.3
  693.1 184.0 %collective-permute-start = (bf16[2,64,64,128]{3,2,1,0:T(8,128)(2,1)S(1)}, bf16[2,64,64,128]{3,2,1,0:T(8,128)(2,1)}, u32[]{:S(2)}, u32[]{:S(2)}) collective-permute-start(bf16[2,64,64,128]{3,2,1,0:T(8,128)(2,1)S(1)} %add_convert_fusion.3), channel_id=1, source_target_pairs={{0,4},{4,8},{8,12},{1,5},{5,9},{9,13},{2,6},{6,10},{10,14},{3,7},{... | collective-permute-start | bytes 6291464 | tf_op jit(solution)/shard_map/while/body/eval_jaxpr/ppermute | solution.py:16
  877.1 43.0 %collective-permute-done = bf16[2,64,64,128]{3,2,1,0:T(8,128)(2,1)} collective-permute-done((bf16[2,64,64,128]{3,2,1,0:T(8,128)(2,1)S(1)}, bf16[2,64,64,128]{3,2,1,0:T(8,128)(2,1)}, u32[]{:S(2)}, u32[]{:S(2)}) %collective-permute-start) | collective-permute-done | bytes 2097184 | tf_op jit(solution)/shard_map/while/body/eval_jaxpr/ppermute | solution.py:16
  920.1 5.9 convert_select_fusion.2
  926.0 4.0 add_convert_fusion.3
  930.0 4.5 collective-permute-start
  934.5 42.1 %collective-permute-done = bf16[2,64,64,128]{3,2,1,0:T(8,128)(2,1)} collective-permute-done((bf16[2,64,64,128]{3,2,1,0:T(8,128)(2,1)S(1)}, bf16[2,64,64,128]{3,2,1,0:T(8,128)(2,1)}, u32[]{:S(2)}, u32[]{:S(2)}) %collective-permute-start) | collective-permute-done | bytes 2097184 | tf_op jit(solution)/shard_map/while/body/eval_jaxpr/ppermute | solution.py:16
  976.7 5.9 convert_select_fusion.2
  982.6 22.4 %fusion.12 = f32[2,1,128,64,64]{2,4,3,0,1:T(8,128)} fusion(f32[2,64,64,128]{3,2,1,0:T(8,128)} %fusion.28, f32[2,64,128,64]{2,3,1,0:T(8,128)} %fusion, f32[2,1,128,64,64]{2,4,3,0,1:T(8,128)} %bitcast.69, f32[2,64,64,128]{3,2,1,0:T(8,128)} %get-tuple-element.76, f32[2,128,64,128]{3,1,2,0:T(8,128)} %bitcast.67, f32[64]{0:T(128)S(1)} %copy-done.8, ...), kind=kOutput, calls=%fused_computation.19 | convolution fusion | flops 1616904192 | bytes 29491456 | tf_op jit(solution)/shard_map/sclhn,shpn->sclhp/dot_general | solution.py:118
  1004.9 5.6 copy.95
  1010.6 5.6 fusion.25
  1016.2 5.3 fusion.40
  1021.6 6.5 mul.183
  1028.0 2.8 reduce_sum.8
  1030.9 2.6 mul.184
  1033.5 6.0 mul.185
  1039.5 42.1 %copy.98 = bf16[4096,4,1024]{2,1,0:T(4,128)(2,1)} copy(bf16[4096,4,1024]{2,0,1:T(8,128)(2,1)} %bitcast.28) | data formatting | bytes 67108864 | tf_op jit(solution)/shard_map/reshape | solution.py:130
  1081.6 54.1 %reshape.230 = bf16[4096,4096,1]{1,0,2:T(8,128)(2,1)} reshape(bf16[4096,4,1024]{2,1,0:T(4,128)(2,1)} %copy.98) | data formatting | bytes 67108864 | tf_op jit(solution)/shard_map/reshape | solution.py:130
  1135.7 19.2 %convolution_convert_fusion = bf16[2,128,4096]{2,1,0:T(8,128)(2,1)} fusion(bf16[4096,4096,1]{1,0,2:T(8,128)(2,1)} %reshape.230, f32[2,128,4096]{2,1,0:T(8,128)} %mul.185, f32[4096]{0:T(1024)S(1)} %copy-done.10, f32[2,128,4096]{2,1,0:T(8,128)} %copy.95, bf16[2,128,4096]{2,1,0:T(8,128)(2,1)S(1)} %copy-done.3), kind=kOutput, calls=%fused_computation.12 | convolution fusion | flops 8600420352 | bytes 46153728 | tf_op jit(solution)/shard_map/stk,kd->std/dot_general | solution.py:127
  1155.0 4.3 dynamic-slice_convert_fusion
  1159.3 3.8 copy.99
  1163.1 24.6 %reduce-scatter.2.cloned.1.call-done = bf16[2,128,2048]{2,1,0:T(8,128)(2,1)} async-done(((bf16[2,128,4096]{2,1,0:T(8,128)(2,1)}), bf16[2,128,2048]{2,1,0:T(8,128)(2,1)}) %reduce-scatter.2.cloned.1.call-update) | async-done | bytes 1048592 | tf_op jit(solution)/shard_map/reduce_scatter | solution.py:135
  1187.6 2.4 multiply_convert_fusion.2
  (57 shorter events, 1.6 us)
Async XLA Ops:
  20.6 1018.9 %all-to-all-start = ((bf16[4,4096,1024]{2,1,0:T(8,128)(2,1)}), bf16[4,4096,1024]{2,1,0:T(8,128)(2,1)}, u32[]{:S(2)}, u32[]{:S(2)}) async-start(bf16[4,4096,1024]{2,1,0:T(8,128)(2,1)} %stack.2), calls=%async_computation | async-start | bytes 67108864 | tf_op jit(solution)/shard_map/all_to_all | solution.py:131
  30.4 4.3 copy-start.1
  30.4 20.9 %all-gather.3.cloned.1.call-start = ((), (), s32[]{:S(2)}) async-start(), calls=%async_computation.2 | async-start | bytes 6291456 | tf_op jit(solution)/shard_map/all_gather | solution.py:55
  34.6 283.0 %all-gather.5.cloned.1.call-start = ((), (), s32[]{:S(2)}) async-start(), calls=%async_computation.3 | async-start | bytes 5242880 | tf_op jit(solution)/shard_map/all_gather | solution.py:60
  37.2 3.0 copy-start.6
  37.2 3.1 copy-start.11
  37.2 3.2 copy-start.12
  37.2 3.3 copy-start.7
  37.2 4.0 copy-start.9
  41.0 14.8 %copy-start.4 = (bf16[2,128,8,128]{3,2,1,0:T(8,128)(2,1)S(1)}, bf16[2,128,8,128]{3,2,1,0:T(8,128)(2,1)}, u32[]{:S(2)}) copy-start(bf16[2,128,8,128]{3,2,1,0:T(8,128)(2,1)} %param.17) | copy-start | bytes 1572868
  41.0 14.8 %copy-start.5 = (bf16[2,128,8,128]{3,2,1,0:T(8,128)(2,1)S(1)}, bf16[2,128,8,128]{3,2,1,0:T(8,128)(2,1)}, u32[]{:S(2)}) copy-start(bf16[2,128,8,128]{3,2,1,0:T(8,128)(2,1)} %param.18) | copy-start | bytes 1572868
  55.5 1099.5 %all-reduce.2.cloned.1.call-start = ((), (), s32[]{:S(2)}) async-start(), calls=%async_computation.5 | async-start | bytes 4194304 | tf_op jit(solution)/shard_map/psum | solution.py:21
  57.6 18.2 %copy-start = (f32[2,128,4,16,128]{4,1,3,2,0:T(8,128)}, f32[2,128,4,16,128]{4,1,3,2,0:T(8,128)S(1)}, u32[]{:S(2)}) copy-start(f32[2,128,4,16,128]{4,1,3,2,0:T(8,128)S(1)} %broadcast_in_dim.68) | copy-start | bytes 25165828
  75.8 1.6 copy-start.2
  327.6 654.9 %copy-start.8 = (f32[64]{0:T(128)S(1)}, f32[64]{0:T(128)}, u32[]{:S(2)}) copy-start(f32[64]{0:T(128)} %param.22) | copy-start | bytes 772
  331.8 351.4 %collective-permute-start = (bf16[2,64,64,128]{3,2,1,0:T(8,128)(2,1)S(1)}, bf16[2,64,64,128]{3,2,1,0:T(8,128)(2,1)}, u32[]{:S(2)}, u32[]{:S(2)}) collective-permute-start(bf16[2,64,64,128]{3,2,1,0:T(8,128)(2,1)S(1)} %add_convert_fusion.3), channel_id=1, source_target_pairs={{0,4},{4,8},{8,12},{1,5},{5,9},{9,13},{2,6},{6,10},{10,14},{3,7},{... | collective-permute-start | bytes 6291464 | tf_op jit(solution)/shard_map/while/body/eval_jaxpr/ppermute | solution.py:16
  693.1 227.0 %collective-permute-start = (bf16[2,64,64,128]{3,2,1,0:T(8,128)(2,1)S(1)}, bf16[2,64,64,128]{3,2,1,0:T(8,128)(2,1)}, u32[]{:S(2)}, u32[]{:S(2)}) collective-permute-start(bf16[2,64,64,128]{3,2,1,0:T(8,128)(2,1)S(1)} %add_convert_fusion.3), channel_id=1, source_target_pairs={{0,4},{4,8},{8,12},{1,5},{5,9},{9,13},{2,6},{6,10},{10,14},{3,7},{... | collective-permute-start | bytes 6291464 | tf_op jit(solution)/shard_map/while/body/eval_jaxpr/ppermute | solution.py:16
  930.0 46.7 %collective-permute-start = (bf16[2,64,64,128]{3,2,1,0:T(8,128)(2,1)S(1)}, bf16[2,64,64,128]{3,2,1,0:T(8,128)(2,1)}, u32[]{:S(2)}, u32[]{:S(2)}) collective-permute-start(bf16[2,64,64,128]{3,2,1,0:T(8,128)(2,1)S(1)} %add_convert_fusion.3), channel_id=1, source_target_pairs={{0,4},{4,8},{8,12},{1,5},{5,9},{9,13},{2,6},{6,10},{10,14},{3,7},{... | collective-permute-start | bytes 6291464 | tf_op jit(solution)/shard_map/while/body/eval_jaxpr/ppermute | solution.py:16
  1010.6 5.7 copy-start.3
  1016.2 171.5 %reduce-scatter.2.cloned.1.call-start = ((), (), s32[]{:S(2)}) async-start(), calls=%async_computation.4 | async-start | bytes 3145728 | tf_op jit(solution)/shard_map/reduce_scatter | solution.py:135
  1081.6 54.1 %copy-start.10 = (f32[4096]{0:T(1024)S(1)}, f32[4096]{0:T(1024)}, u32[]{:S(2)}) copy-start(f32[4096]{0:T(1024)} %param.23) | copy-start | bytes 49156
Sparse Core Ops, SparseCore 0:
  34.8 16.5 all-gather.2
  55.6 261.9 all-gather.4
  1016.3 86.7 all-reduce.1
  1155.1 32.4 reduce-scatter.1
